TPU v7x, 32 devices: a whole 2x2x4 slice. The times are simulated.
32 devices in a mesh: row: 8 (over z, x), col: 4 (over y, core).
Axes of the slice: x: 2, y: 2, z: 4, core: 2. Of those that a mesh axis runs over, the one named last changes fastest.
Arguments:
- events: bfloat16 [2048, 256], P(('row', 'col')), may hold values from -6 to 6
- timestamps: int32 [2048], replicated, may hold values from 0 to 8384512, as said below
- norm_gain: float32 [256], replicated, may hold values from 0.1 to 1.9
- w_in: bfloat16 [256, 1024], replicated, may hold values from -0.375 to 0.375
- rel_bias: float32 [2, 24], replicated, may hold values from -2 to 2
- out_gain: float32 [256], replicated, may hold values from 0.1 to 1.9
- w_out: bfloat16 [256, 256], replicated, may hold values from -0.75 to 0.75
Outputs:
- output: bfloat16 [2048, 256], P(('row', 'col'))
Inputs may be any that keep to these rules, and one draw needn't show every extreme that they name: `timestamps`: nondecreasing along the events, the first one 0 and the last one 4096 * 2047.
All inputs are finite; a program needn't handle non-finite values.
Results may differ from a plain program's by a relative error of at most 0.006.
Values may be sent and summed in bfloat16 or wider, within the bound.
A program may use at most 64 MiB of HBM per device.

v0:
```python
import functools
import math

import jax
import jax.numpy as jnp
from jax import lax
from jax.experimental import pallas as pl
from jax.experimental.pallas import tpu as pltpu
from jax.sharding import PartitionSpec as P

HEAD = 128
NEAR = 2
LANES = 128
MESH = pl.DeviceIdType.MESH


def layer_norm(values, gain):
    center = values - jnp.mean(values, axis=-1, keepdims=True)
    variance = jnp.mean(center * center, axis=-1, keepdims=True)
    return center * lax.rsqrt(variance + 1e-05) * gain


def silu(values):
    half = 0.5 * values
    return half + half * jnp.tanh(half)


def dot(a, b):
    return jnp.dot(a, b, preferred_element_type=jnp.float32)


def kernel(
    fold, n_rows, n_cols, ev, ts_in, norm_gain_in, w_in_in, rel_bias_in, out_gain_in, w_out_in, out,
    ts, norm_gain, w_in, rel_bias, out_gain, w_out, load_sem, kv_buf, q_buf, red_buf, send_buf, q_all, q_times, acc, table, gate,
    ready, row_send, row_recv, col_send, col_recv, red_send, red_recv,
):
    axis_row, axis_cols = lax.axis_index("row"), n_cols // fold
    my_row, inner = axis_row // fold, lax.rem(axis_row, fold)
    my_col = inner * axis_cols + lax.axis_index("col")
    local, width = q_buf.shape[1:]
    heads, buckets = rel_bias.shape
    block = local * n_cols
    group = LANES // local
    tile = min(block, 512)
    near = NEAR if axis_cols % NEAR == 0 else 1
    half_scale = 0.5 / math.sqrt(HEAD)

    def in_col(r):
        return {"row": r * fold + inner}

    def in_row(c):
        return {"row": my_row * fold + c // axis_cols, "col": lax.rem(c, axis_cols)}

    barrier = pltpu.get_barrier_semaphore()

    def greet(semaphore, target):
        pl.semaphore_signal(semaphore, inc=1, device_id=target, device_id_type=MESH)

    beside = (my_row > 0) * 1 + (my_row < n_rows - 1) * 1
    part_cols = axis_cols // near
    my_part = my_col // near
    far = [
        lax.rem(inner + i, fold) * part_cols + lax.rem(my_part % part_cols + j, part_cols)
        for i in range(fold) for j in range(part_cols) if i + j > 0
    ]
    mates = [my_part * near + lax.rem(my_col % near + step, near) for step in range(1, near)]
    others = mates + [q * near + k for q in far for k in range(near)]

    @pl.when(my_row > 0)
    def _():
        greet(barrier, in_col(my_row - 1))

    @pl.when(my_row < n_rows - 1)
    def _():
        greet(barrier, in_col(my_row + 1))

    for c in others:
        greet(barrier, in_row(c))

    loads = [
        pltpu.make_async_copy(source, target, load_sem.at[i])
        for i, (source, target) in enumerate([
            (ev, q_buf.at[my_col]), (ev, kv_buf.at[my_row]), (norm_gain_in, norm_gain),
            (w_in_in, w_in), (rel_bias_in, rel_bias), (ts_in, ts),
            (out_gain_in, out_gain), (w_out_in, w_out),
        ])
    ]
    for load in loads:
        load.start()
    loads[0].wait()
    pl.semaphore_wait(barrier, beside + n_cols - 1)

    def row_copy(slot, r):
        return pltpu.make_async_remote_copy(
            src_ref=q_buf.at[my_col], dst_ref=kv_buf.at[slot], send_sem=row_send.at[r],
            recv_sem=row_recv.at[slot], device_id=in_col(r), device_id_type=MESH,
        )

    def col_copy(slot, c):
        return pltpu.make_async_remote_copy(
            src_ref=q_buf.at[my_col], dst_ref=q_buf.at[slot], send_sem=col_send.at[c],
            recv_sem=col_recv.at[slot], device_id=in_row(c), device_id_type=MESH,
        )

    def red_copy(slot, c):
        return pltpu.make_async_remote_copy(
            src_ref=send_buf.at[c], dst_ref=red_buf.at[slot], send_sem=red_send.at[c],
            recv_sem=red_recv.at[slot], device_id=in_row(c), device_id_type=MESH,
        )

    def start_row(i, carry):
        row_copy(my_row, n_rows - 1 - i).start()
        return carry

    @pl.when(my_row < n_rows - 1)
    def _():
        row_copy(my_row, my_row + 1).start()

    for c in mates + others[:len(mates) - 1:-1]:
        col_copy(my_col, c).start()

    @pl.when(my_row < n_rows - 2)
    def _():
        pl.semaphore_wait(ready, 1)

    @pl.when((my_row > 0) & (my_row < n_rows - 1))
    def _():
        greet(ready, in_col(my_row - 1))

    lax.fori_loop(0, n_rows - 2 - my_row, start_row, 0)

    for load in loads[1:]:
        load.wait()
    own = q_buf[my_col]
    lead = my_row // group * group
    for g in range(group):
        r = lead + g

        @pl.when(r > my_row)
        def _():
            kv_buf[r] = jnp.zeros_like(own)

    normed = layer_norm(own.astype(jnp.float32), norm_gain[...]).astype(jnp.bfloat16)
    gate[...] = silu(dot(normed, w_in[:, :width])).astype(jnp.bfloat16)

    lane = lax.broadcasted_iota(jnp.int32, (heads, LANES), 1)
    table[:, :buckets] = rel_bias[...]
    table[...] = 0.5 * jnp.where(lane < buckets, table[...], rel_bias[:, buckets - 1 :])
    for i in range(block // LANES):
        stamps = ts[pl.ds(my_row * (block // LANES) + i, 1), :]
        q_times[pl.ds(i * LANES, LANES), :] = jnp.broadcast_to(stamps, (LANES, LANES)).T

    def members(q):
        return mates if q is my_part else [q * near + k for k in range(near)]

    def project_queries(q):
        for c in members(q):
            col_copy(c, c).wait_recv()
        size = near * local
        rows = q_buf[pl.ds(q * near, near)].reshape(size, width).astype(jnp.float32)
        normed_q = layer_norm(rows, norm_gain[...]).astype(jnp.bfloat16)
        q_all[pl.ds(pl.multiple_of(q * size, size), size), :] = silu(
            dot(normed_q, w_in[:, width : 2 * width])
        ).astype(jnp.bfloat16)

    def each_tile(body):
        if block == tile:
            body(0)
        else:
            lax.fori_loop(0, block // tile, lambda i, carry: (body(i), carry)[1], 0)

    def chunk(c):
        return acc[pl.ds(pl.multiple_of(c * local, local), local), :]

    def send_sum(c):
        send_buf[c] = chunk(c).astype(jnp.bfloat16)
        red_copy(my_col, c).start()

    def attend(p, diagonal, tail=False):
        first = p * group
        for g in range(group):
            r = first + g
            if diagonal:

                @pl.when(r < my_row)
                def _():
                    row_copy(r, r).wait_recv()

            else:
                row_copy(r, r).wait_recv()
        rows = kv_buf[pl.ds(first, group)].reshape(LANES, width).astype(jnp.float32)
        normed_kv = layer_norm(rows, norm_gain[...]).astype(jnp.bfloat16)
        pair = silu(dot(normed_kv, w_in[:, 2 * width :])).astype(jnp.bfloat16)
        spot = lax.broadcasted_iota(jnp.int32, (1, LANES), 1)
        key_times = jnp.zeros((1, LANES), jnp.int32)
        for g in range(group):
            begin = (first + g) * block + my_col * local
            stamps = ts[pl.ds(begin // LANES, 1), :]
            shift = lax.rem(g * local - begin % LANES + LANES, LANES)
            stamps = pltpu.roll(jnp.broadcast_to(stamps, (8, LANES)), shift, 1)[:1]
            key_times = jnp.where(spot // local == g, stamps, key_times)

        def one_tile(i, size=tile):
            begin = i * size
            if not isinstance(i, int):
                begin = pl.multiple_of(begin, size)
            here = pl.ds(begin, size)
            delta = q_times[here, :] - key_times
            bucket = 32 - lax.clz(delta)
            if diagonal:
                key_pos = (first + spot // local) * block + my_col * local + spot % local
                query_pos = (
                    my_row * block + begin
                    + lax.broadcasted_iota(jnp.int32, (size, LANES), 0)
                )
                causal = query_pos >= key_pos
            for h in range(heads):
                cols = slice(h * HEAD, (h + 1) * HEAD)
                values = slice(width + h * HEAD, width + (h + 1) * HEAD)
                bias = jnp.take_along_axis(
                    jnp.broadcast_to(table[h : h + 1, :], (size, LANES)), bucket, axis=1,
                    mode="promise_in_bounds",
                )
                scores = lax.dot_general(
                    q_all[here, cols], pair[:, cols],
                    (((1,), (1,)), ((), ())), preferred_element_type=jnp.float32,
                )
                half = scores * half_scale + bias
                weights = half + half * jnp.tanh(half)
                if diagonal:
                    weights = jnp.where(causal, weights, 0.0)
                update = dot(weights.astype(jnp.bfloat16), pair[:, values])
                if diagonal:
                    acc[here, cols] = update
                else:
                    acc[here, cols] += update

        if diagonal:
            for q in [my_part] + far:
                project_queries(q)
                one_tile(q, near * local)

                @pl.when(my_row < group)
                def _():
                    for c in members(q):
                        send_sum(c)
        elif tail:
            for q in far[::-1] + [my_part]:
                one_tile(q, near * local)
                for c in members(q):
                    send_sum(c)
        else:
            each_tile(one_tile)

    last_group = my_row // group
    attend(last_group, True)

    def one_group(i, carry):
        attend(last_group - 1 - i, False)
        return carry

    lax.fori_loop(0, last_group - 1, one_group, 0)

    @pl.when(last_group > 0)
    def _():
        attend(0, False, tail=True)

    total = chunk(my_col)
    for c in others:
        red_copy(c, c).wait_recv()
        total = total + red_buf[c].astype(jnp.float32)
    mixed = layer_norm(total, out_gain[...]) * gate[...].astype(jnp.float32)
    out[...] = (
        q_buf[my_col].astype(jnp.float32) + dot(mixed.astype(jnp.bfloat16), w_out[...])
    ).astype(jnp.bfloat16)

    def end_row(i, carry):
        row_copy(my_row, n_rows - 1 - i).wait_send()
        return carry

    lax.fori_loop(0, n_rows - 1 - my_row, end_row, 0)
    for c in others:
        col_copy(my_col, c).wait_send()
        red_copy(my_col, c).wait_send()


def solution(mesh):
    fold = 2 if mesh.shape["row"] % 4 == 0 else 1
    n_rows, n_cols = mesh.shape["row"] // fold, mesh.shape["col"] * fold

    def on_device(events, timestamps, norm_gain, w_in, rel_bias, out_gain, w_out):
        local, width = events.shape
        block = local * n_cols
        heads = rel_bias.shape[0]
        vmem = pl.BlockSpec(memory_space=pltpu.VMEM)
        dma = pltpu.SemaphoreType.DMA
        return pl.pallas_call(
            functools.partial(kernel, fold, n_rows, n_cols),
            out_shape=jax.ShapeDtypeStruct((local, width), jnp.bfloat16),
            in_specs=[pl.BlockSpec(memory_space=pl.ANY)] * 7,
            out_specs=vmem,
            scratch_shapes=[
                pltpu.VMEM((timestamps.shape[0] // LANES, LANES), jnp.int32),
                pltpu.VMEM((1, width), jnp.float32),
                pltpu.VMEM(w_in.shape, w_in.dtype),
                pltpu.VMEM(rel_bias.shape, rel_bias.dtype),
                pltpu.VMEM((1, width), jnp.float32),
                pltpu.VMEM(w_out.shape, w_out.dtype),
                dma((8,)),
                pltpu.VMEM((n_rows, local, width), jnp.bfloat16),
                pltpu.VMEM((n_cols, local, width), jnp.bfloat16),
                pltpu.VMEM((n_cols, local, width), jnp.bfloat16),
                pltpu.VMEM((n_cols, local, width), jnp.bfloat16),
                pltpu.VMEM((block, width), jnp.bfloat16),
                pltpu.VMEM((block, LANES), jnp.int32),
                pltpu.VMEM((block, width), jnp.float32),
                pltpu.VMEM((heads, LANES), jnp.float32),
                pltpu.VMEM((local, width), jnp.bfloat16),
                pltpu.SemaphoreType.REGULAR,
                dma((n_rows,)), dma((n_rows,)),
                dma((n_cols,)), dma((n_cols,)),
                dma((n_cols,)), dma((n_cols,)),
            ],
            compiler_params=pltpu.CompilerParams(collective_id=0, has_side_effects=True),
        )(
            events,
            timestamps.reshape(-1, LANES),
            norm_gain.reshape(1, -1),
            w_in,
            rel_bias,
            out_gain.reshape(1, -1),
            w_out,
        )

    return jax.shard_map(
        on_device,
        mesh=mesh,
        in_specs=(P(("row", "col"), None), P(), P(), P(), P(), P(), P()),
        out_specs=P(("row", "col"), None),
        check_vma=False,
    )
```

profile of v0, /device:TPU:17, one launch (start us, length us, event | category | flops | bytes accessed | tf_op | source)
XLA Modules:
  0.0 16.7 jit_solution(13420035837165067753)
XLA Ops:
  0.0 15.4 %shard_map.73 = bf16[64,256]{1,0:T(8,128)(2,1)} custom-call(bf16[64,256]{1,0:T(8,128)(2,1)} %ev.1, s32[16,128]{1,0:T(8,128)} %bitcast.3, f32[1,256]{1,0:T(1,128)} %bitcast.4, bf16[256,1024]{1,0:T(8,128)(2,1)} %w_in_in.1, f32[2,24]{1,0:T(2,128)} %rel_bias_in.1, f32[1,256]{1,0:T(1,128)} %bitcast.5, bf16[256,256]{1,0:T(8,128)(2,1)} %w_out_in.1), custom_call_target="tpu_custom_call" | custom-call | tf_op jit(solution)/shard_map/pallas_call | solution.py:297
  15.4 1.4 %copy.9 = bf16[64,256]{1,0:T(8,128)(2,1)} copy(bf16[64,256]{1,0:T(8,128)(2,1)} %shard_map.73) | data formatting | bytes 65536
where the time goes:
time: 16.9 us; the launch traced here: 16.7 us
  Pallas kernels  15.4 us (91%)
  local copies, waits for them, and re-layouts  1.38 us (8%)
    pallas_call x1, Pallas kernels, on_device(): pl.pallas_call(functools.partial(kernel, fold, n_rows, n_cols), out_shape...  15.4 us
    unnamed x1, local copies, waits for them, and re-layouts  1.38 us

commit v1 on v0

--- a/solution.py
+++ b/solution.py
@@ -296,7 +296,7 @@
         dma = pltpu.SemaphoreType.DMA
         return pl.pallas_call(
             functools.partial(kernel, fold, n_rows, n_cols),
-            out_shape=jax.ShapeDtypeStruct((local, width), jnp.bfloat16),
+            out_shape=pltpu.VMEM((local, width), jnp.bfloat16),
             in_specs=[pl.BlockSpec(memory_space=pl.ANY)] * 7,
             out_specs=vmem,
             scratch_shapes=[

time: 16.9 us -> 15.5 us (0.917)
  local copies, waits for them, and re-layouts: 1.38 us -> 0.62 us
  Pallas kernels: 15.4 us -> 14.8 us
    unnamed x1, local copies, waits for them, and re-layouts: 1.38 us -> 0.62 us
    pallas_call x1, Pallas kernels: 15.4 us -> 14.8 us  [on_device(): pl.pallas_call(functools.partial(kernel, fold, n_rows, n_cols), out_shape...]
where the time goes in v1:
time: 15.5 us; the launch traced here: 15.4 us
  Pallas kernels  14.8 us (95%)
  local copies, waits for them, and re-layouts  0.62 us (4%)
    pallas_call x1, Pallas kernels, on_device(): pl.pallas_call(functools.partial(kernel, fold, n_rows, n_cols), out_shape...  14.8 us
    unnamed x1, local copies, waits for them, and re-layouts  0.62 us

profile of v1, /device:TPU:17, one launch (start us, length us, event | category | flops | bytes accessed | tf_op | source)
XLA Modules:
  0.0 15.4 jit_solution(7832145875348851279)
XLA Ops:
  0.0 14.8 %shard_map.73 = bf16[64,256]{1,0:T(8,128)(2,1)S(1)} custom-call(bf16[64,256]{1,0:T(8,128)(2,1)} %ev.1, s32[16,128]{1,0:T(8,128)} %bitcast.3, f32[1,256]{1,0:T(1,128)} %bitcast.4, bf16[256,1024]{1,0:T(8,128)(2,1)} %w_in_in.1, f32[2,24]{1,0:T(2,128)} %rel_bias_in.1, f32[1,256]{1,0:T(1,128)} %bitcast.5, bf16[256,256]{1,0:T(8,128)(2,1)} %w_out_in.1), custom_call_target="tpu_custom_call" | custom-call | tf_op jit(solution)/shard_map/pallas_call | solution.py:297
  14.8 0.6 %copy.9 = bf16[64,256]{1,0:T(8,128)(2,1)} copy(bf16[64,256]{1,0:T(8,128)(2,1)S(1)} %shard_map.73) | data formatting | bytes 65536

commit v2 on v1

v2 whole, which is shorter than its diff:
```python
import functools
import math

import jax
import jax.numpy as jnp
from jax import lax
from jax.experimental import pallas as pl
from jax.experimental.pallas import tpu as pltpu
from jax.sharding import PartitionSpec as P

HEAD = 128
CORES = 2
LANES = 128
MESH = pl.DeviceIdType.MESH


def layer_norm(values, gain):
    center = values - jnp.mean(values, axis=-1, keepdims=True)
    variance = jnp.mean(center * center, axis=-1, keepdims=True)
    return center * lax.rsqrt(variance + 1e-05) * gain


def silu(values):
    half = 0.5 * values
    return half + half * jnp.tanh(half)


def dot(a, b):
    return jnp.dot(a, b, preferred_element_type=jnp.float32)


def kernel(
    fold, n_rows, n_cols, ev, ts_in, norm_gain_in, w_in_in, rel_bias_in, out_gain_in, w_out_in, out,
    raw, ts, norm_gain, w_in, rel_bias, out_gain, w_out, load_sem,
    plane_buf, query_buf, red_buf, send_buf, pair_buf, q_times, total, table, gate, ready,
    plane_send, plane_recv, hand_send, hand_recv, query_send, query_recv, red_send, red_recv,
):
    axis_row, axis_col = lax.axis_index("row"), lax.axis_index("col")
    n_chips = n_cols // CORES
    side = n_chips // fold
    plane, inner = axis_row // fold, lax.rem(axis_row, fold)
    core, place = lax.rem(axis_col, CORES), axis_col // CORES
    other = 1 - core
    chip = inner * side + place
    local, width = raw.shape
    heads, buckets = rel_bias.shape
    later_planes, later_chips = n_rows - 1 - plane, n_chips - 1 - chip
    group = min(n_chips, 4)
    half_scale = 0.5 / math.sqrt(HEAD)

    peers = [
        lax.rem(inner + i, fold) * side + lax.rem(place + j, side)
        for i in range(fold) for j in range(side) if i + j > 0
    ]

    def in_plane(i):
        return {"row": plane * fold + i // side, "col": lax.rem(i, side) * CORES + other}

    def in_column(r):
        return {"row": r * fold + inner, "col": place * CORES + other}

    partner = {"row": axis_row, "col": place * CORES + other}

    def each(count, body):
        lax.fori_loop(0, count, lambda i, carry: (body(i), carry)[1], 0)

    barrier = pltpu.get_barrier_semaphore()

    def greet(semaphore, target):
        pl.semaphore_signal(semaphore, inc=1, device_id=target, device_id_type=MESH)

    each(later_planes, lambda i: greet(barrier, in_column(n_rows - 1 - i)))
    each(later_chips, lambda i: greet(barrier, in_plane(n_chips - 1 - i)))
    greet(barrier, partner)

    loads = [
        pltpu.make_async_copy(source, target, load_sem.at[i])
        for i, (source, target) in enumerate([
            (ev, raw), (norm_gain_in, norm_gain), (ts_in, ts), (rel_bias_in, rel_bias), (w_in_in, w_in),
            (out_gain_in, out_gain), (w_out_in, w_out),
        ])
    ]
    for load in loads:
        load.start()

    def remote(source, target, send_sem, recv_sem, device):
        return pltpu.make_async_remote_copy(
            src_ref=source, dst_ref=target, send_sem=send_sem, recv_sem=recv_sem,
            device_id=device, device_id_type=MESH,
        )

    mine = plane_buf.at[chip, core]

    def plane_copy(slot, i):
        return remote(mine, plane_buf.at[slot, core], plane_send.at[i], plane_recv.at[slot], in_plane(i))

    def query_copy(slot, r):
        return remote(mine, query_buf.at[slot], query_send.at[r], query_recv.at[slot], in_column(r))

    own_hand = remote(mine, mine, hand_send.at[chip], hand_recv.at[chip], partner)

    def hand(i):
        return remote(plane_buf.at[i, other], plane_buf.at[i, other], hand_send.at[i], hand_recv.at[i], partner)

    def red_copy(slot, r):
        return remote(send_buf.at[r], red_buf.at[slot], red_send.at[r], red_recv.at[slot], in_column(r))

    pl.semaphore_wait(barrier, plane + chip + 1)
    each(chip, lambda i: greet(ready, in_plane(i)))

    loads[0].wait()
    loads[1].wait()
    own = layer_norm(raw[...].astype(jnp.float32), norm_gain[...]).astype(jnp.bfloat16)
    plane_buf[chip, core] = own

    each(plane, lambda r: query_copy(plane, r).start())
    each(chip, lambda i: plane_copy(chip, i).start())
    own_hand.start()

    for load in loads[2:4]:
        load.wait()

    lane = lax.broadcasted_iota(jnp.int32, (heads, LANES), 1)
    table[:, :buckets] = rel_bias[...]
    table[...] = 0.5 * jnp.where(lane < buckets, table[...], rel_bias[:, buckets - 1 :])

    def stamps_of(r, i):
        return ts[pl.ds(r * n_chips + i, 1), :]

    def fill_times(r, part):
        stamps = jnp.broadcast_to(stamps_of(r, chip), (LANES, LANES)).T
        q_times[r] = jnp.where(part > 0, stamps[local:], stamps[:local])

    fill_times(plane, core)
    each(later_planes, lambda i: fill_times(plane + 1 + i, other))

    @pl.when(later_chips > 0)
    def _():
        pl.semaphore_wait(ready, later_chips)

    each(later_chips, lambda i: plane_copy(chip, n_chips - 1 - i).start())

    for load in loads[4:]:
        load.wait()

    def project_query(rows):
        return silu(dot(rows, w_in[:, width : 2 * width])).astype(jnp.bfloat16)

    def project_pair(i):
        rows = pl.ds(pl.multiple_of(i * LANES, LANES), LANES)
        block = plane_buf[i].reshape(LANES, width)
        pair_buf[rows, :] = silu(dot(block, w_in[:, 2 * width :])).astype(jnp.bfloat16)

    def attend(query, times, causal):
        def keys(first):
            rows = pl.ds(pl.multiple_of(first * LANES, LANES), group * LANES)
            buckets_of = [32 - lax.clz(times - stamps_of(plane, first + i)) for i in range(group)]
            if causal:
                query_pos = chip * LANES + core * local + lax.broadcasted_iota(jnp.int32, (local, group * LANES), 0)
                key_pos = first * LANES + lax.broadcasted_iota(jnp.int32, (local, group * LANES), 1)
            parts = []
            for h in range(heads):
                cols = slice(h * HEAD, (h + 1) * HEAD)
                values = slice(width + h * HEAD, width + (h + 1) * HEAD)
                row = jnp.broadcast_to(table[h : h + 1, :], (local, LANES))
                bias = jnp.concatenate([
                    jnp.take_along_axis(row, bucket, axis=1, mode="promise_in_bounds")
                    for bucket in buckets_of
                ], axis=1)
                scores = lax.dot_general(
                    query[:, cols], pair_buf[rows, cols],
                    (((1,), (1,)), ((), ())), preferred_element_type=jnp.float32,
                )
                half = scores * half_scale + bias
                weights = half + half * jnp.tanh(half)
                if causal:
                    weights = jnp.where(query_pos >= key_pos, weights, 0.0)
                parts.append(dot(weights.astype(jnp.bfloat16), pair_buf[rows, values]))
            return jnp.concatenate(parts, axis=1)

        if group == n_chips:
            return keys(0)
        return lax.fori_loop(
            0, n_chips // group, lambda g, sums: sums + keys(g * group),
            jnp.zeros((local, width), jnp.float32),
        )

    own_query = project_query(own)
    gate[...] = silu(dot(own, w_in[:, :width])).astype(jnp.bfloat16)

    own_hand.wait_recv()
    project_pair(chip)
    for i in peers:
        plane_copy(i, i).wait_recv()
        hand(i).start()
    for i in peers:
        hand(i).wait_recv()
        project_pair(i)

    def serve(i):
        r = plane + 1 + i
        query_copy(r, r).wait_recv()
        query = project_query(query_buf[r])
        send_buf[r] = attend(query, q_times[r], False).astype(jnp.bfloat16)
        red_copy(plane, r).start()

    each(later_planes, serve)
    total[...] = attend(own_query, q_times[plane], True)

    def gather(r):
        red_copy(r, r).wait_recv()
        total[...] += red_buf[r].astype(jnp.float32)

    each(plane, gather)

    mixed = layer_norm(total[...], out_gain[...]) * gate[...].astype(jnp.float32)
    out[...] = (
        raw[...].astype(jnp.float32) + dot(mixed.astype(jnp.bfloat16), w_out[...])
    ).astype(jnp.bfloat16)

    own_hand.wait_send()
    for i in peers:
        plane_copy(chip, i).wait_send()
        hand(i).wait_send()
    each(plane, lambda r: query_copy(plane, r).wait_send())
    each(later_planes, lambda i: red_copy(plane, plane + 1 + i).wait_send())


def solution(mesh):
    fold = 2 if mesh.shape["row"] % 4 == 0 else 1
    n_rows, n_cols = mesh.shape["row"] // fold, mesh.shape["col"] * fold
    n_chips = n_cols // CORES

    def on_device(events, timestamps, norm_gain, w_in, rel_bias, out_gain, w_out):
        local, width = events.shape
        if local * CORES != LANES or mesh.shape["col"] % CORES:
            raise ValueError("unsupported sizes")
        heads = rel_bias.shape[0]
        vmem = pl.BlockSpec(memory_space=pltpu.VMEM)
        dma = pltpu.SemaphoreType.DMA
        return pl.pallas_call(
            functools.partial(kernel, fold, n_rows, n_cols),
            out_shape=pltpu.VMEM((local, width), jnp.bfloat16),
            in_specs=[pl.BlockSpec(memory_space=pl.ANY)] * 7,
            out_specs=vmem,
            scratch_shapes=[
                pltpu.VMEM((local, width), jnp.bfloat16),
                pltpu.VMEM((timestamps.shape[0] // LANES, LANES), jnp.int32),
                pltpu.VMEM((1, width), jnp.float32),
                pltpu.VMEM(w_in.shape, w_in.dtype),
                pltpu.VMEM(rel_bias.shape, rel_bias.dtype),
                pltpu.VMEM((1, width), jnp.float32),
                pltpu.VMEM(w_out.shape, w_out.dtype),
                dma((7,)),
                pltpu.VMEM((n_chips, CORES, local, width), jnp.bfloat16),
                pltpu.VMEM((n_rows, local, width), jnp.bfloat16),
                pltpu.VMEM((n_rows, local, width), jnp.bfloat16),
                pltpu.VMEM((n_rows, local, width), jnp.bfloat16),
                pltpu.VMEM((n_chips * LANES, 2 * width), jnp.bfloat16),
                pltpu.VMEM((n_rows, local, LANES), jnp.int32),
                pltpu.VMEM((local, width), jnp.float32),
                pltpu.VMEM((heads, LANES), jnp.float32),
                pltpu.VMEM((local, width), jnp.bfloat16),
                pltpu.SemaphoreType.REGULAR,
                dma((n_chips,)), dma((n_chips,)), dma((n_chips,)), dma((n_chips,)),
                dma((n_rows,)), dma((n_rows,)), dma((n_rows,)), dma((n_rows,)),
            ],
            compiler_params=pltpu.CompilerParams(collective_id=0, has_side_effects=True),
        )(
            events,
            timestamps.reshape(-1, LANES),
            norm_gain.reshape(1, -1),
            w_in,
            rel_bias,
            out_gain.reshape(1, -1),
            w_out,
        )

    return jax.shard_map(
        on_device,
        mesh=mesh,
        in_specs=(P(("row", "col"), None), P(), P(), P(), P(), P(), P()),
        out_specs=P(("row", "col"), None),
        check_vma=False,
    )
```

time: 15.5 us -> 13.4 us (0.86)
  the two profiles are of different devices: /device:TPU:17 before, /device:TPU:27 now
where the time goes in v2:
time: 13.4 us; the launch traced here: 13.2 us
  Pallas kernels  12.6 us (94%)
  local copies, waits for them, and re-layouts  0.62 us (5%)
    pallas_call x1, Pallas kernels, on_device(): pl.pallas_call(functools.partial(kernel, fold, n_rows, n_cols), out_shape...  12.6 us
    unnamed x1, local copies, waits for them, and re-layouts  0.62 us

profile of v2, /device:TPU:27, one launch (start us, length us, event | category | flops | bytes accessed | tf_op | source)
XLA Modules:
  0.0 13.2 jit_solution(3492800864293943135)
XLA Ops:
  0.0 12.6 %shard_map.73 = bf16[64,256]{1,0:T(8,128)(2,1)S(1)} custom-call(bf16[64,256]{1,0:T(8,128)(2,1)} %ev.1, s32[16,128]{1,0:T(8,128)} %bitcast.3, f32[1,256]{1,0:T(1,128)} %bitcast.4, bf16[256,1024]{1,0:T(8,128)(2,1)} %w_in_in.1, f32[2,24]{1,0:T(2,128)} %rel_bias_in.1, f32[1,256]{1,0:T(1,128)} %bitcast.5, bf16[256,256]{1,0:T(8,128)(2,1)} %w_out_in.1), custom_call_target="tpu_custom_call" | custom-call | tf_op jit(solution)/shard_map/pallas_call | solution.py:241
  12.6 0.6 %copy.9 = bf16[64,256]{1,0:T(8,128)(2,1)} copy(bf16[64,256]{1,0:T(8,128)(2,1)S(1)} %shard_map.73) | data formatting | bytes 65536

commit v3 on v2

--- a/solution.py
+++ b/solution.py
@@ -44,7 +44,7 @@
     chip = inner * side + place
     local, width = raw.shape
     heads, buckets = rel_bias.shape
-    later_planes, later_chips = n_rows - 1 - plane, n_chips - 1 - chip
+    later_planes = n_rows - 1 - plane
     group = min(n_chips, 4)
     half_scale = 0.5 / math.sqrt(HEAD)
 
@@ -53,11 +53,11 @@
         for i in range(fold) for j in range(side) if i + j > 0
     ]
 
-    def in_plane(i):
-        return {"row": plane * fold + i // side, "col": lax.rem(i, side) * CORES + other}
-
-    def in_column(r):
-        return {"row": r * fold + inner, "col": place * CORES + other}
+    def in_plane(i, member=other):
+        return {"row": plane * fold + i // side, "col": lax.rem(i, side) * CORES + member}
+
+    def in_column(r, member=other):
+        return {"row": r * fold + inner, "col": place * CORES + member}
 
     partner = {"row": axis_row, "col": place * CORES + other}
 
@@ -69,9 +69,13 @@
     def greet(semaphore, target):
         pl.semaphore_signal(semaphore, inc=1, device_id=target, device_id_type=MESH)
 
-    each(later_planes, lambda i: greet(barrier, in_column(n_rows - 1 - i)))
-    each(later_chips, lambda i: greet(barrier, in_plane(n_chips - 1 - i)))
-    greet(barrier, partner)
+    for i in peers[::-1]:
+        greet(barrier, in_plane(i, 1))
+    each(later_planes, lambda i: greet(barrier, in_column(n_rows - 1 - i, 0)))
+
+    @pl.when(core == 1)
+    def _():
+        greet(barrier, partner)
 
     loads = [
         pltpu.make_async_copy(source, target, load_sem.at[i])
@@ -105,17 +109,34 @@
     def red_copy(slot, r):
         return remote(send_buf.at[r], red_buf.at[slot], red_send.at[r], red_recv.at[slot], in_column(r))
 
-    pl.semaphore_wait(barrier, plane + chip + 1)
-    each(chip, lambda i: greet(ready, in_plane(i)))
+    @pl.when(core == 0)
+    def _():
+        pl.semaphore_wait(barrier, CORES * plane + 1)
+        greet(ready, partner)
 
     loads[0].wait()
     loads[1].wait()
     own = layer_norm(raw[...].astype(jnp.float32), norm_gain[...]).astype(jnp.bfloat16)
     plane_buf[chip, core] = own
 
+    @pl.when(core == 1)
+    def _():
+        pl.semaphore_wait(ready, 1)
+
     each(plane, lambda r: query_copy(plane, r).start())
-    each(chip, lambda i: plane_copy(chip, i).start())
     own_hand.start()
+
+    @pl.when(core == 1)
+    def _():
+        pl.semaphore_wait(barrier, CORES * (n_chips - 1))
+        greet(ready, partner)
+
+    @pl.when(core == 0)
+    def _():
+        pl.semaphore_wait(ready, 1)
+
+    for i in peers[::-1]:
+        plane_copy(chip, i).start()
 
     for load in loads[2:4]:
         load.wait()
@@ -133,12 +154,6 @@
 
     fill_times(plane, core)
     each(later_planes, lambda i: fill_times(plane + 1 + i, other))
-
-    @pl.when(later_chips > 0)
-    def _():
-        pl.semaphore_wait(ready, later_chips)
-
-    each(later_chips, lambda i: plane_copy(chip, n_chips - 1 - i).start())
 
     for load in loads[4:]:
         load.wait()
@@ -204,7 +219,11 @@
         send_buf[r] = attend(query, q_times[r], False).astype(jnp.bfloat16)
         red_copy(plane, r).start()
 
-    each(later_planes, serve)
+    @pl.when(later_planes > 0)
+    def _():
+        serve(later_planes - 1)
+
+    each(later_planes - 1, serve)
     total[...] = attend(own_query, q_times[plane], True)
 
     def gather(r):

time: 13.4 us -> 13 us (0.970)
  the two profiles are of different devices: /device:TPU:27 before, /device:TPU:21 now
where the time goes in v3:
time: 13 us; the launch traced here: 12.8 us
  Pallas kernels  12.2 us (94%)
  local copies, waits for them, and re-layouts  0.62 us (5%)
    pallas_call x1, Pallas kernels, on_device(): pl.pallas_call(functools.partial(kernel, fold, n_rows, n_cols), out_shape...  12.2 us
    unnamed x1, local copies, waits for them, and re-layouts  0.62 us

profile of v3, /device:TPU:21, one launch (start us, length us, event | category | flops | bytes accessed | tf_op | source)
XLA Modules:
  0.0 12.8 jit_solution(5410055190210791935)
XLA Ops:
  0.0 12.2 %shard_map.73 = bf16[64,256]{1,0:T(8,128)(2,1)S(1)} custom-call(bf16[64,256]{1,0:T(8,128)(2,1)} %ev.1, s32[16,128]{1,0:T(8,128)} %bitcast.3, f32[1,256]{1,0:T(1,128)} %bitcast.4, bf16[256,1024]{1,0:T(8,128)(2,1)} %w_in_in.1, f32[2,24]{1,0:T(2,128)} %rel_bias_in.1, f32[1,256]{1,0:T(1,128)} %bitcast.5, bf16[256,256]{1,0:T(8,128)(2,1)} %w_out_in.1), custom_call_target="tpu_custom_call" | custom-call | tf_op jit(solution)/shard_map/pallas_call | solution.py:260
  12.2 0.6 %copy.9 = bf16[64,256]{1,0:T(8,128)(2,1)} copy(bf16[64,256]{1,0:T(8,128)(2,1)S(1)} %shard_map.73) | data formatting | bytes 65536

commit v4 on v3

--- a/solution.py
+++ b/solution.py
@@ -80,7 +80,7 @@
     loads = [
         pltpu.make_async_copy(source, target, load_sem.at[i])
         for i, (source, target) in enumerate([
-            (ev, raw), (norm_gain_in, norm_gain), (ts_in, ts), (rel_bias_in, rel_bias), (w_in_in, w_in),
+            (ev, raw), (norm_gain_in, norm_gain), (w_in_in, w_in), (ts_in, ts), (rel_bias_in, rel_bias),
             (out_gain_in, out_gain), (w_out_in, w_out),
         ])
     ]
@@ -99,7 +99,7 @@
         return remote(mine, plane_buf.at[slot, core], plane_send.at[i], plane_recv.at[slot], in_plane(i))
 
     def query_copy(slot, r):
-        return remote(mine, query_buf.at[slot], query_send.at[r], query_recv.at[slot], in_column(r))
+        return remote(query_buf.at[plane], query_buf.at[slot], query_send.at[r], query_recv.at[slot], in_column(r))
 
     own_hand = remote(mine, mine, hand_send.at[chip], hand_recv.at[chip], partner)
 
@@ -123,9 +123,13 @@
     def _():
         pl.semaphore_wait(ready, 1)
 
+    def project_query(rows):
+        return silu(dot(rows, w_in[:, width : 2 * width])).astype(jnp.bfloat16)
+
+    own_hand.start()
+    loads[2].wait()
+    query_buf[plane] = project_query(own)
     each(plane, lambda r: query_copy(plane, r).start())
-    own_hand.start()
-
     @pl.when(core == 1)
     def _():
         pl.semaphore_wait(barrier, CORES * (n_chips - 1))
@@ -138,7 +142,7 @@
     for i in peers[::-1]:
         plane_copy(chip, i).start()
 
-    for load in loads[2:4]:
+    for load in loads[3:5]:
         load.wait()
 
     lane = lax.broadcasted_iota(jnp.int32, (heads, LANES), 1)
@@ -155,11 +159,8 @@
     fill_times(plane, core)
     each(later_planes, lambda i: fill_times(plane + 1 + i, other))
 
-    for load in loads[4:]:
+    for load in loads[5:]:
         load.wait()
-
-    def project_query(rows):
-        return silu(dot(rows, w_in[:, width : 2 * width])).astype(jnp.bfloat16)
 
     def project_pair(i):
         rows = pl.ds(pl.multiple_of(i * LANES, LANES), LANES)
@@ -200,7 +201,6 @@
             jnp.zeros((local, width), jnp.float32),
         )
 
-    own_query = project_query(own)
     gate[...] = silu(dot(own, w_in[:, :width])).astype(jnp.bfloat16)
 
     own_hand.wait_recv()
@@ -215,8 +215,7 @@
     def serve(i):
         r = plane + 1 + i
         query_copy(r, r).wait_recv()
-        query = project_query(query_buf[r])
-        send_buf[r] = attend(query, q_times[r], False).astype(jnp.bfloat16)
+        send_buf[r] = attend(query_buf[r], q_times[r], False).astype(jnp.bfloat16)
         red_copy(plane, r).start()
 
     @pl.when(later_planes > 0)
@@ -224,7 +223,7 @@
         serve(later_planes - 1)
 
     each(later_planes - 1, serve)
-    total[...] = attend(own_query, q_times[plane], True)
+    total[...] = attend(query_buf[plane], q_times[plane], True)
 
     def gather(r):
         red_copy(r, r).wait_recv()

time: 13 us -> 12.7 us (0.977)
  Pallas kernels: 12.2 us -> 12 us
    pallas_call x1, Pallas kernels: 12.2 us -> 12 us  [on_device(): pl.pallas_call(functools.partial(kernel, fold, n_rows, n_cols), out_shape...]
where the time goes in v4:
time: 12.7 us; the launch traced here: 12.6 us
  Pallas kernels  12 us (94%)
  local copies, waits for them, and re-layouts  0.62 us (5%)
    pallas_call x1, Pallas kernels, on_device(): pl.pallas_call(functools.partial(kernel, fold, n_rows, n_cols), out_shape...  12 us
    unnamed x1, local copies, waits for them, and re-layouts  0.62 us

profile of v4, /device:TPU:21, one launch (start us, length us, event | category | flops | bytes accessed | tf_op | source)
XLA Modules:
  0.0 12.6 jit_solution(15202415653069272098)
XLA Ops:
  0.0 12.0 %shard_map.73 = bf16[64,256]{1,0:T(8,128)(2,1)S(1)} custom-call(bf16[64,256]{1,0:T(8,128)(2,1)} %ev.1, s32[16,128]{1,0:T(8,128)} %bitcast.3, f32[1,256]{1,0:T(1,128)} %bitcast.4, bf16[256,1024]{1,0:T(8,128)(2,1)} %w_in_in.1, f32[2,24]{1,0:T(2,128)} %rel_bias_in.1, f32[1,256]{1,0:T(1,128)} %bitcast.5, bf16[256,256]{1,0:T(8,128)(2,1)} %w_out_in.1), custom_call_target="tpu_custom_call" | custom-call | tf_op jit(solution)/shard_map/pallas_call | solution.py:259
  12.0 0.6 %copy.9 = bf16[64,256]{1,0:T(8,128)(2,1)} copy(bf16[64,256]{1,0:T(8,128)(2,1)S(1)} %shard_map.73) | data formatting | bytes 65536
